TPU v7x, 32 devices: a whole 2x2x4 slice. The times are simulated.
32 devices in a mesh: diamond: 2 (over x), tile: 16 (over z, y, core).
Axes of the slice: x: 2, y: 2, z: 4, core: 2. Of those that a mesh axis runs over, the one named last changes fastest.
Arguments:
- inputs: bfloat16 [128, 64, 2048], P(None, 'diamond', 'tile'), may hold values from -6 to 6
- cotangent: bfloat16 [128, 64, 2048], P(None, 'diamond', 'tile'), may hold values from -6 to 6
- weight: bfloat16 [7, 128, 128], replicated, may hold values from -0.1875 to 0.1875
- bias: float32 [128], replicated, may hold values from -4 to 4
- ocean: int32 [4, 128], P('diamond', 'tile'), may hold values 0 or 1
Outputs:
- grad_inputs: bfloat16 [128, 64, 2048], P(None, 'diamond', 'tile')
- grad_weight: float32 [7, 128, 128], replicated
- grad_bias: float32 [128], replicated
All inputs are finite; a program needn't handle non-finite values. No bound on the sum of `ocean` on one device may be relied on, other than what follows from the above.
Results may differ from a plain program's by a relative error of at most 0.005.
Values may be sent and summed in bfloat16 or wider, within the bound.
A program may use at most 128 MiB of HBM per device.

v0:
```python
import jax
import jax.numpy as jnp
from jax import lax
from jax.sharding import PartitionSpec as P

BLOCK = 16


OFFSETS = ((0, 0), (0, 1), (0, -1), (1, 0), (-1, 0), (1, -1), (-1, 1))


def extended(value, sides, width):
    for axis, dim in sides:
        size, length = (lax.axis_size(axis), value.shape[dim])
        up = [(i, (i + 1) % size) for i in range(size - 1)]
        down = [(j, i) for i, j in up]
        last = lax.slice_in_dim(value, length - width, length, axis=dim)
        initial = lax.slice_in_dim(value, 0, width, axis=dim)
        before = lax.ppermute(last, axis, up)
        after = lax.ppermute(initial, axis, down)
        value = jnp.concatenate([before, value, after], axis=dim)
    return value


def stacked_taps(padded, rows, cols, sign, base):
    pieces = [
        padded[
            :,
            base + sign * dr : base + sign * dr + rows,
            base + sign * dc : base + sign * dc + cols,
        ]
        for dr, dc in OFFSETS
    ]
    return jnp.stack(pieces, 0)


def pre_grad(taps, weight, bias, grad_here, mask_here):
    feats = weight.shape[1]
    shape_here = grad_here.shape
    flat = taps.reshape(7 * feats, -1)
    pre = (
        lax.dot_general(
            weight.reshape(7 * feats, feats),
            flat,
            (((0,), (0,)), ((), ())),
            preferred_element_type=jnp.float32,
        )
        + bias[:, None]
    )
    sig = jax.nn.sigmoid(pre)
    result = (
        mask_here.reshape(1, -1)
        * grad_here.reshape(feats, -1).astype(jnp.float32)
        * sig
        * (1.0 + pre * (1.0 - sig))
    )
    return result.astype(jnp.bfloat16).reshape(shape_here)


def on_device(inputs, cotangent, weight, bias, ocean):
    feats, rows, cols = inputs.shape
    total_cells = rows * cols * lax.axis_size("diamond") * lax.axis_size("tile")
    scale = total_cells ** (-0.5)
    cell_mask = jnp.repeat(jnp.repeat(ocean.astype(jnp.float32), BLOCK, 0), BLOCK, 1)
    back_weight = jnp.transpose(weight, (1, 0, 2)).reshape(feats, 7 * feats)
    x_pad = extended(inputs, (("diamond", 1), ("tile", 2)), 1)
    taps = stacked_taps(x_pad, rows, cols, 1, 1)
    grad_pre = pre_grad(taps, weight, bias, cotangent, cell_mask)
    taps_inner = taps.reshape(7 * feats, rows * cols)
    grad_inner = grad_pre.reshape(feats, rows * cols)
    grad_region = extended(grad_pre, (("diamond", 1), ("tile", 2)), 1)
    local_w = lax.dot_general(
        taps_inner, grad_inner, (((1,), (1,)), ((), ())), preferred_element_type=jnp.float32
    )
    local_b = jnp.sum(grad_inner.astype(jnp.float32), axis=1)
    sum_w, sum_b = lax.psum((local_w, local_b), ("diamond", "tile"))
    back_taps = stacked_taps(grad_region, rows, cols, -1, 1).reshape(7 * feats, rows * cols)
    total = jnp.dot(back_weight, back_taps, preferred_element_type=jnp.float32)
    grad_inputs = (
        (cotangent.reshape(feats, rows * cols).astype(jnp.float32) + total)
        .astype(jnp.bfloat16)
        .reshape(feats, rows, cols)
    )
    grad_weight = (sum_w * scale).reshape(7, feats, feats)
    grad_bias = sum_b * scale
    return (grad_inputs, grad_weight, grad_bias)


def solution(mesh):
    placed = (
        P(None, "diamond", "tile"),
        P(None, "diamond", "tile"),
        P(),
        P(),
        P("diamond", "tile"),
    )
    return jax.shard_map(
        on_device,
        mesh=mesh,
        in_specs=placed,
        out_specs=(P(None, "diamond", "tile"), P(), P()),
        check_vma=False,
    )
```

profile of v0, /device:TPU:1, one launch (start us, length us, event | category | flops | bytes accessed | tf_op | source)
XLA Modules:
  0.0 196.3 jit_solution(1103404638283157046)
XLA Ops:
  7.2 2.6 %copy.46 = bf16[128,32,128]{0,1,2:T(8,128)(2,1)S(1)} copy(bf16[128,32,128]{2,1,0:T(8,128)(2,1)} %param.5) | data formatting | bytes 2097152 | tf_op args[0]
  10.5 3.9 %collective-permute-start = (bf16[128,1,128]{0,1,2:T(2,128)(2,1)}, bf16[128,1,128]{0,1,2:T(2,128)(2,1)S(1)}, u32[]{:S(2)}, u32[]{:S(2)}) collective-permute-start(bf16[128,1,128]{0,1,2:T(2,128)(2,1)} %get-tuple-element.25), channel_id=1, source_target_pairs={{0,16},{1,17},{2,18},{3,19},{4,20},{5,21},{6,22},{7,23},{8,24},{9,... | collective-permute-start | bytes 98312 | tf_op jit(solution)/shard_map/ppermute | solution.py:19
  18.4 1.9 copy.44
  22.1 2.9 %collective-permute-start.2 = (bf16[128,34,1]{0,1,2:T(8,128)(2,1)S(1)}, bf16[128,34,1]{0,1,2:T(8,128)(2,1)S(1)}, u32[]{:S(2)}, u32[]{:S(2)}) collective-permute-start(bf16[128,34,1]{0,1,2:T(8,128)(2,1)S(1)} %get-tuple-element.22), channel_id=1, source_target_pairs={{1,0},{2,1},{3,2},{4,3},{5,4},{6,5},{7,6},{8,7},{9,8},{10,9},{11,1... | collective-permute-start | bytes 26120 | tf_op jit(solution)/shard_map/ppermute | solution.py:20
  25.4 3.0 %collective-permute-start.3 = (bf16[128,34,1]{0,1,2:T(8,128)(2,1)S(1)}, bf16[128,34,1]{0,1,2:T(8,128)(2,1)S(1)}, u32[]{:S(2)}, u32[]{:S(2)}) collective-permute-start(bf16[128,34,1]{0,1,2:T(8,128)(2,1)S(1)} %get-tuple-element.21), channel_id=1, source_target_pairs={{0,1},{1,2},{2,3},{3,4},{4,5},{5,6},{6,7},{7,8},{8,9},{9,10},{10,1... | collective-permute-start | bytes 26120 | tf_op jit(solution)/shard_map/ppermute | solution.py:19
  28.5 1.4 fusion.50
  33.3 1.4 fusion.45
  34.7 1.3 fusion.43
  36.0 12.3 %copy.57 = bf16[7,128,32,128]{3,2,1,0:T(8,128)(2,1)} copy(bf16[7,128,32,128]{1,3,2,0:T(8,128)(2,1)} %fusion.43) | data formatting | bytes 14680064 | tf_op jit(solution)/shard_map/stack | solution.py:34
  48.3 6.6 %convert_reduce_fusion = (f32[128]{0:T(128)S(1)}, bf16[128,4096]{0,1:T(8,128)(2,1)S(1)}) fusion(f32[128]{0:T(128)S(1)} %copy-done.8, bf16[896,128]{1,0:T(8,128)(2,1)S(1)} %bitcast.116, bf16[112,8,32,128]{3,2,1,0:T(8,128)(2,1)} %bitcast.110, f32[128,32,128]{0,2,1:T(8,128)S(1)} %copy-done.2, f32[4096]{0:T(1024)S(1)} %mul.31), kind=kOutput, calls=%fused_computation.18 | convolution fusion | flops 946339712 | bytes 10732544 | tf_op jit(solution)/shard_map/dot_general | solution.py:42
  55.0 2.9 %fusion.3 = f32[896,128]{1,0:T(8,128)} fusion(bf16[128,4096]{0,1:T(8,128)(2,1)S(1)} %get-tuple-element.28, bf16[112,8,32,128]{3,2,1,0:T(8,128)(2,1)S(1)} %bitcast.111), kind=kOutput, calls=%fused_computation.3 | convolution fusion | flops 939524096 | bytes 8847360 | tf_op jit(solution)/shard_map/dot_general | solution.py:72
  58.7 4.3 %collective-permute-start.4 = (bf16[128,1,128]{0,1,2:T(2,128)(2,1)S(1)}, bf16[128,1,128]{0,1,2:T(2,128)(2,1)S(1)}, u32[]{:S(2)}, u32[]{:S(2)}) collective-permute-start(bf16[128,1,128]{0,1,2:T(2,128)(2,1)S(1)} %get-tuple-element.23), channel_id=1, source_target_pairs={{0,16},{1,17},{2,18},{3,19},{4,20},{5,21},{6,22},{7,23},{8,24},{9,... | collective-permute-start | bytes 98312 | tf_op jit(solution)/shard_map/ppermute | solution.py:19
  64.3 41.4 %psum.15 = f32[128]{0:T(128)S(1)} all-reduce(f32[128]{0:T(128)S(1)} %get-tuple-element.27), channel_id=1, replica_groups=mesh['diamond'=2,'tile'=16] {'diamond','tile'}, use_global_device_ids=true, to_apply=%region_2.0 | all-reduce | flops 128 | bytes 1024 | tf_op jit(solution)/shard_map/psum | solution.py:76
  108.1 5.1 %collective-permute-start.6 = (bf16[128,34,1]{0,1,2:T(8,128)(2,1)S(1)}, bf16[128,34,1]{0,1,2:T(8,128)(2,1)S(1)}, u32[]{:S(2)}, u32[]{:S(2)}) collective-permute-start(bf16[128,34,1]{0,1,2:T(8,128)(2,1)S(1)} %get-tuple-element.20), channel_id=1, source_target_pairs={{0,1},{1,2},{2,3},{3,4},{4,5},{5,6},{6,7},{7,8},{8,9},{9,10},{10,1... | collective-permute-start | bytes 26120 | tf_op jit(solution)/shard_map/ppermute | solution.py:19
  113.5 1.9 collective-permute-start.7
  115.5 1.4 fusion.31
  116.9 2.0 %collective-permute-done.7 = bf16[128,34,1]{0,1,2:T(8,128)(2,1)S(1)} collective-permute-done((bf16[128,34,1]{0,1,2:T(8,128)(2,1)S(1)}, bf16[128,34,1]{0,1,2:T(8,128)(2,1)S(1)}, u32[]{:S(2)}, u32[]{:S(2)}) %collective-permute-start.7) | collective-permute-done | bytes 8736 | tf_op jit(solution)/shard_map/ppermute | solution.py:20
  119.0 1.4 fusion.42
  122.4 1.4 fusion.37
  125.1 12.4 %copy.67 = bf16[7,128,32,128]{3,2,1,0:T(8,128)(2,1)} copy(bf16[7,128,32,128]{1,3,2,0:T(8,128)(2,1)} %fusion.36) | data formatting | bytes 14680064 | tf_op jit(solution)/shard_map/stack | solution.py:34
  137.5 9.5 %fusion.21 = bf16[128,4096]{0,1:T(8,128)(2,1)S(1)} fusion(f32[128,4096]{0,1:T(8,128)S(1)} %bitcast.113, bf16[128,896]{0,1:T(8,128)(2,1)S(1)} %bitcast.117, bf16[112,8,32,128]{3,2,1,0:T(8,128)(2,1)} %bitcast.112), kind=kOutput, calls=%fused_computation.13 | convolution fusion | flops 940572672 | bytes 10715136 | tf_op jit(solution)/shard_map/dot_general | solution.py:78
  147.0 1.7 copy.69
  148.7 38.9 %all-reduce.2.cloned.1.call-done = f32[896,128]{1,0:T(8,128)} async-done(((f32[896,128]{1,0:T(8,128)}), f32[896,128]{1,0:T(8,128)}) %all-reduce.2.cloned.1.call-update) | async-done | bytes 458768 | tf_op jit(solution)/shard_map/psum | solution.py:76
  187.6 1.8 broadcast_multiply_fusion
  (61 shorter events, 18.7 us)
Async XLA Ops:
  7.2 8.6 %copy-start.1 = (bf16[128,32,128]{2,1,0:T(8,128)(2,1)S(1)}, bf16[128,32,128]{2,1,0:T(8,128)(2,1)}, u32[]{:S(2)}) copy-start(bf16[128,32,128]{2,1,0:T(8,128)(2,1)} %param.5) | copy-start | bytes 3145732
  7.2 180.5 %all-reduce.2.cloned.1.call-start = ((), (), s32[]{:S(2)}) async-start(), calls=%async_computation | async-start | bytes 917504 | tf_op jit(solution)/shard_map/psum | solution.py:76
  10.5 10.8 %collective-permute-start = (bf16[128,1,128]{0,1,2:T(2,128)(2,1)}, bf16[128,1,128]{0,1,2:T(2,128)(2,1)S(1)}, u32[]{:S(2)}, u32[]{:S(2)}) collective-permute-start(bf16[128,1,128]{0,1,2:T(2,128)(2,1)} %get-tuple-element.25), channel_id=1, source_target_pairs={{0,16},{1,17},{2,18},{3,19},{4,20},{5,21},{6,22},{7,23},{8,24},{9,... | collective-permute-start | bytes 98312 | tf_op jit(solution)/shard_map/ppermute | solution.py:19
  14.5 6.9 %collective-permute-start.1 = (bf16[128,1,128]{0,1,2:T(2,128)(2,1)}, bf16[128,1,128]{0,1,2:T(2,128)(2,1)S(1)}, u32[]{:S(2)}, u32[]{:S(2)}) collective-permute-start(bf16[128,1,128]{0,1,2:T(2,128)(2,1)} %get-tuple-element.26), channel_id=1, source_target_pairs={{16,0},{17,1},{18,2},{19,3},{20,4},{21,5},{22,6},{23,7},{24,8},{25... | collective-permute-start | bytes 98312 | tf_op jit(solution)/shard_map/ppermute | solution.py:20
  16.8 1.6 copy-start.4
  16.8 3.5 %copy-start.7 = (s32[2,8]{1,0:T(2,128)S(1)}, s32[2,8]{1,0:T(2,128)}, u32[]{:S(2)}) copy-start(s32[2,8]{1,0:T(2,128)} %param.9) | copy-start | bytes 196
  18.4 2.1 %copy-start.5 = (bf16[7,128,128]{2,1,0:T(8,128)(2,1)S(1)}, bf16[7,128,128]{2,1,0:T(8,128)(2,1)}, u32[]{:S(2)}) copy-start(bf16[7,128,128]{2,1,0:T(8,128)(2,1)} %param.7) | copy-start | bytes 688132
  22.1 6.3 %collective-permute-start.2 = (bf16[128,34,1]{0,1,2:T(8,128)(2,1)S(1)}, bf16[128,34,1]{0,1,2:T(8,128)(2,1)S(1)}, u32[]{:S(2)}, u32[]{:S(2)}) collective-permute-start(bf16[128,34,1]{0,1,2:T(8,128)(2,1)S(1)} %get-tuple-element.22), channel_id=1, source_target_pairs={{1,0},{2,1},{3,2},{4,3},{5,4},{6,5},{7,6},{8,7},{9,8},{10,9},{11,1... | collective-permute-start | bytes 26120 | tf_op jit(solution)/shard_map/ppermute | solution.py:20
  25.4 4.5 %collective-permute-start.3 = (bf16[128,34,1]{0,1,2:T(8,128)(2,1)S(1)}, bf16[128,34,1]{0,1,2:T(8,128)(2,1)S(1)}, u32[]{:S(2)}, u32[]{:S(2)}) collective-permute-start(bf16[128,34,1]{0,1,2:T(8,128)(2,1)S(1)} %get-tuple-element.21), channel_id=1, source_target_pairs={{0,1},{1,2},{2,3},{3,4},{4,5},{5,6},{6,7},{7,8},{8,9},{9,10},{10,1... | collective-permute-start | bytes 26120 | tf_op jit(solution)/shard_map/ppermute | solution.py:19
  36.0 12.3 %copy-start.2 = (f32[128,32,128]{0,2,1:T(8,128)S(1)}, f32[128,32,128]{0,2,1:T(8,128)}, u32[]{:S(2)}) copy-start(f32[128,32,128]{0,2,1:T(8,128)} %copy.44) | copy-start | bytes 6291460
  36.0 12.3 %copy-start.8 = (f32[128]{0:T(128)S(1)}, f32[128]{0:T(128)}, u32[]{:S(2)}) copy-start(f32[128]{0:T(128)} %param.8) | copy-start | bytes 1540
  48.3 6.6 %copy-start = (bf16[7,128,32,128]{3,2,1,0:T(8,128)(2,1)S(1)}, bf16[7,128,32,128]{3,2,1,0:T(8,128)(2,1)}, u32[]{:S(2)}) copy-start(bf16[7,128,32,128]{3,2,1,0:T(8,128)(2,1)} %copy.57) | copy-start | bytes 22020100
  58.7 48.6 %collective-permute-start.4 = (bf16[128,1,128]{0,1,2:T(2,128)(2,1)S(1)}, bf16[128,1,128]{0,1,2:T(2,128)(2,1)S(1)}, u32[]{:S(2)}, u32[]{:S(2)}) collective-permute-start(bf16[128,1,128]{0,1,2:T(2,128)(2,1)S(1)} %get-tuple-element.23), channel_id=1, source_target_pairs={{0,16},{1,17},{2,18},{3,19},{4,20},{5,21},{6,22},{7,23},{8,24},{9,... | collective-permute-start | bytes 98312 | tf_op jit(solution)/shard_map/ppermute | solution.py:19
  63.0 44.3 %collective-permute-start.5 = (bf16[128,1,128]{0,1,2:T(2,128)(2,1)S(1)}, bf16[128,1,128]{0,1,2:T(2,128)(2,1)S(1)}, u32[]{:S(2)}, u32[]{:S(2)}) collective-permute-start(bf16[128,1,128]{0,1,2:T(2,128)(2,1)S(1)} %get-tuple-element.24), channel_id=1, source_target_pairs={{16,0},{17,1},{18,2},{19,3},{20,4},{21,5},{22,6},{23,7},{24,8},{25... | collective-permute-start | bytes 98312 | tf_op jit(solution)/shard_map/ppermute | solution.py:20
  108.1 7.4 %collective-permute-start.6 = (bf16[128,34,1]{0,1,2:T(8,128)(2,1)S(1)}, bf16[128,34,1]{0,1,2:T(8,128)(2,1)S(1)}, u32[]{:S(2)}, u32[]{:S(2)}) collective-permute-start(bf16[128,34,1]{0,1,2:T(8,128)(2,1)S(1)} %get-tuple-element.20), channel_id=1, source_target_pairs={{0,1},{1,2},{2,3},{3,4},{4,5},{5,6},{6,7},{7,8},{8,9},{9,10},{10,1... | collective-permute-start | bytes 26120 | tf_op jit(solution)/shard_map/ppermute | solution.py:19
  113.5 5.4 %collective-permute-start.7 = (bf16[128,34,1]{0,1,2:T(8,128)(2,1)S(1)}, bf16[128,34,1]{0,1,2:T(8,128)(2,1)S(1)}, u32[]{:S(2)}, u32[]{:S(2)}) collective-permute-start(bf16[128,34,1]{0,1,2:T(8,128)(2,1)S(1)} %get-tuple-element.19), channel_id=1, source_target_pairs={{1,0},{2,1},{3,2},{4,3},{5,4},{6,5},{7,6},{8,7},{9,8},{10,9},{11,1... | collective-permute-start | bytes 26120 | tf_op jit(solution)/shard_map/ppermute | solution.py:20
  125.1 12.4 %copy-start.3 = (f32[128,32,128]{0,2,1:T(8,128)S(1)}, f32[128,32,128]{0,2,1:T(8,128)}, u32[]{:S(2)}) copy-start(f32[128,32,128]{0,2,1:T(8,128)} %copy.44) | copy-start | bytes 6291460
  125.1 12.4 %copy-start.6 = (bf16[7,128,128]{1,2,0:T(8,128)(2,1)S(1)}, bf16[7,128,128]{1,2,0:T(8,128)(2,1)}, u32[]{:S(2)}) copy-start(bf16[7,128,128]{1,2,0:T(8,128)(2,1)} %copy.68) | copy-start | bytes 688132
Sparse Core Ops, SparseCore 0:
  58.0 129.5 all-reduce.1
where the time goes:
time: 197 us; the launch traced here: 196 us
  local copies, waits for them, and re-layouts  43.3 us (22%)
  blocking collectives  41.4 us (21%)
  waiting for transfers between devices  41 us (21%)
  starting transfers between devices  23.7 us (12%)
  matrix products  19 us (10%)
  between operations  14.3 us (7%)
  other arithmetic  13.6 us (7%)
    psum x1, blocking collectives, on_device(): sum_w, sum_b = lax.psum((local_w, local_b), ('diamond', 'tile'))  41.4 us
    psum x1, waiting for transfers between devices, on_device(): sum_w, sum_b = lax.psum((local_w, local_b), ('diamond', 'tile'))  38.9 us
    another operation x3, local copies, waits for them, and re-layouts, stacked_taps(): return jnp.stack(pieces, 0)  26 us
    ppermute x4, starting transfers between devices, extended(): before = lax.ppermute(last, axis, up)  16.3 us
    unnamed x29, local copies, waits for them, and re-layouts  13.6 us
    dot_general x1, matrix products, on_device(): total = jnp.dot(back_weight, back_taps, preferred_element_type=jnp.float32)  9.47 us
    unnamed x7, other arithmetic  8.35 us
    ppermute x4, starting transfers between devices, extended(): after = lax.ppermute(initial, axis, down)  7.37 us
  transfers between devices with their start and end apart: 9, of which 2 were waited for; matrix products, arithmetic and copies ran while one was open for 21% of the time, Pallas kernels for 0%

commit v1 on v0

v1 whole, which is shorter than its diff:
```python
import functools

import jax
import jax.numpy as jnp
from jax import lax
from jax.experimental import pallas as pl
from jax.experimental.pallas import tpu as pltpu
from jax.sharding import PartitionSpec as P

BLOCK = 16
LANES = 128
FORWARD = (1, 0, 2, 6, 4, 3, 5)
BACKWARD = (2, 0, 1, 5, 3, 4, 6)
MESH = pl.DeviceIdType.MESH
UP, DOWN, LEFT, RIGHT, UPRIGHT, LOWLEFT = range(6)
SUMMED = 32
f32, bf16 = jnp.float32, jnp.bfloat16


def kernel(D, T, R, F, summed, x_hbm, c_hbm, w_hbm, b_ref, m_ref, y_hbm, a_hbm,
           xv, cv, wv, xf, cf, xs, gs, wt, wb, bb, bacc, x_cols, g_cols, xh, gh,
           total, s1, r1, s2, r2, full, in_sem, xss, xrs, gss, grs, pair_sem, rs_s, rs_r, ag_s, ag_r):
    C = LANES
    d = lax.axis_index("diamond")
    t = lax.axis_index("tile")
    ins = [pltpu.make_async_copy(a, b, in_sem.at[i])
           for i, (a, b) in enumerate(((x_hbm, xv), (w_hbm, wv), (c_hbm, cv)))]
    for copy in ins:
        copy.start()

    up, down, left, right = d > 0, d < D - 1, t > 0, t < T - 1
    sends = (
        (down, (d + 1, t), UP, 1),
        (up, (d - 1, t), DOWN, 0),
        (right, (d, t + 1), LEFT, 3),
        (left, (d, t - 1), RIGHT, 2),
        (jnp.logical_and(down, left), (d + 1, t - 1), UPRIGHT, 2),
        (jnp.logical_and(up, right), (d - 1, t + 1), LOWLEFT, 3),
    )
    filled = (up, down, left, right, jnp.logical_and(up, right), jnp.logical_and(down, left))

    barrier = pltpu.get_barrier_semaphore()
    if summed:
        me = d * T + t
        for s in range(1, D * T):
            p = lax.rem(me + s, D * T)
            pl.semaphore_signal(barrier, inc=1, device_id=(p // T, p % T), device_id_type=MESH)
    else:
        for there, device, _, _ in sends:
            @pl.when(there)
            def _():
                pl.semaphore_signal(barrier, inc=1, device_id=device, device_id_type=MESH)

    lane = lax.broadcasted_iota(jnp.int32, (F, C), 1)

    def at(r):
        return pl.ds(pl.multiple_of(r * C, C), C)

    def spread(source, target):
        @pl.loop(0, F // 8)
        def _(i):
            f = pl.multiple_of(i * 8, 8)
            target[pl.ds(pl.multiple_of(i * 8 * R, 8 * R), 8 * R), :] = (
                source[pl.ds(f, 8)].reshape(8 * R, C).astype(f32))

    def columns(value, r, cols):
        cols[0] = jnp.where(lane == r, pltpu.roll(value, r, 1), cols[0])
        cols[1] = jnp.where(lane == r, pltpu.roll(value, r + 1, 1), cols[1])

    def halo_copies(stack, edge, halo, ssem, rsem):
        pieces = (stack.at[F:2 * F, C:2 * C], stack.at[F:2 * F, R * C:(R + 1) * C], edge.at[0], edge.at[1])
        return [(there, pltpu.make_async_remote_copy(
            src_ref=pieces[piece], dst_ref=halo.at[slot], send_sem=ssem.at[slot], recv_sem=rsem.at[slot],
            device_id=device, device_id_type=MESH)) for there, device, slot, piece in sends]

    def start(copies):
        for there, copy in copies:
            @pl.when(there)
            def _():
                copy.start()

    def finish(copies, stack, halo):
        for there, copy in copies:
            @pl.when(there)
            def _():
                copy.wait_send()
        for slot in range(6):
            @pl.when(filled[slot])
            def _():
                copies[slot][1].wait_recv()

            @pl.when(jnp.logical_not(filled[slot]))
            def _():
                halo[slot] = jnp.zeros((F, C), bf16)
        above, below = halo[UP], halo[DOWN]
        stack[F:2 * F, 0:C] = above
        stack[F:2 * F, (R + 1) * C:(R + 2) * C] = below
        corner = pltpu.roll(halo[UPRIGHT].astype(f32), C - R, 1)
        stack[0:F, 0:C] = jnp.where(lane == C - 1, corner, pltpu.roll(above.astype(f32), C - 1, 1)).astype(bf16)
        corner = halo[LOWLEFT].astype(f32)
        stack[2 * F:3 * F, (R + 1) * C:(R + 2) * C] = jnp.where(
            lane == 0, corner, pltpu.roll(below.astype(f32), 1, 1)).astype(bf16)

        @pl.loop(0, R)
        def _(r):
            value = stack[F:2 * F, at(r + 1)].astype(f32)
            after = pltpu.roll(halo[RIGHT].astype(f32), C - 1 - r, 1)
            before = pltpu.roll(halo[LEFT].astype(f32), lax.rem(C - r, C), 1)
            stack[0:F, at(r + 1)] = jnp.where(lane == C - 1, after, pltpu.roll(value, C - 1, 1)).astype(bf16)
            stack[2 * F:3 * F, at(r + 1)] = jnp.where(lane == 0, before, pltpu.roll(value, 1, 1)).astype(bf16)

    def conv(weights, stack, r, rows):
        def some(r):
            return pl.ds(pl.multiple_of(r * C, C), rows * C)
        out = jnp.dot(weights[:, 0:3 * F], stack[:, some(r + 1)], preferred_element_type=f32)
        out += jnp.dot(weights[:, 3 * F:5 * F], stack[0:2 * F, some(r)], preferred_element_type=f32)
        return out + jnp.dot(weights[:, 5 * F:7 * F], stack[F:3 * F, some(r + 2)], preferred_element_type=f32)

    ins[0].wait()
    spread(xv, xf)

    @pl.loop(0, R)
    def _(r):
        value = xf[pl.ds(r, F, stride=R), :]
        xs[F:2 * F, at(r + 1)] = value.astype(bf16)
        columns(value, r, x_cols[0])

    x_cols[1][...] = x_cols[0][...].astype(bf16)
    if summed:
        pl.semaphore_wait(barrier, D * T - 1)
    else:
        for there in filled:
            @pl.when(there)
            def _():
                pl.semaphore_wait(barrier, 1)
    x_copies = halo_copies(xs, x_cols[1], xh, xss, xrs)
    start(x_copies)

    ins[1].wait()
    for slot, (k, j) in enumerate(zip(FORWARD, BACKWARD)):
        wt[:, slot * F:(slot + 1) * F] = wv[k].astype(f32).T.astype(bf16)
        wb[:, slot * F:(slot + 1) * F] = wv[j]
    bb[...] = jnp.broadcast_to(b_ref[...], (F, F)).T
    bacc[...] = jnp.zeros_like(bacc)
    ins[2].wait()
    spread(cv, cf)
    finish(x_copies, xs, xh)

    step = 4

    @pl.loop(0, R // step)
    def _(i):
        pre = conv(wt, xs, i * step, step)
        mask = m_ref[pl.ds(i * step // BLOCK, 1), :]
        for j in range(step):
            r = i * step + j
            z = pre[:, j * C:(j + 1) * C] + bb[...]
            s = 0.5 + 0.5 * jnp.tanh(0.5 * z)
            g = (mask * cf[pl.ds(r, F, stride=R), :] * s * (1.0 + z * (1.0 - s))).astype(bf16)
            gs[F:2 * F, at(r + 1)] = g
            g = g.astype(f32)
            bacc[...] += g
            columns(g, r, g_cols[0])

    g_cols[1][...] = g_cols[0][...].astype(bf16)
    g_copies = halo_copies(gs, g_cols[1], gh, gss, grs)
    start(g_copies)

    wide = 8
    total[...] = jnp.zeros_like(total)

    @pl.loop(0, R // wide)
    def _(i):
        def some(r):
            return pl.ds(pl.multiple_of(r * C, C), wide * C)
        r = i * wide
        g = gs[F:2 * F, some(r + 1)]
        for first, many, rows, row in ((0, 3, slice(0, 3 * F), r + 1), (3, 2, slice(0, 2 * F), r), (5, 2, slice(F, 3 * F), r + 2)):
            part = lax.dot_general(xs[rows, some(row)], g, (((1,), (1,)), ((), ())), preferred_element_type=f32)
            for j in range(many):
                k = FORWARD[first + j]
                total[k * F:(k + 1) * F, :] += part[j * F:(j + 1) * F, :]

    total[7 * F:8 * F, :] = jnp.broadcast_to(jnp.sum(bacc[...].T, axis=0, keepdims=True), (F, F))

    def back(first, last):
        @pl.loop(first, last)
        def _(i):
            part = conv(wb, gs, i * step, step)
            for j in range(step):
                r = i * step + j
                xf[pl.ds(r, F, stride=R), :] = part[:, j * C:(j + 1) * C] + cf[pl.ds(r, F, stride=R), :]

    def put():
        @pl.loop(0, F // 8)
        def _(i):
            f = pl.multiple_of(i * 8, 8)
            xv[pl.ds(f, 8)] = xf[pl.ds(pl.multiple_of(i * 8 * R, 8 * R), 8 * R), :].astype(bf16).reshape(8, R, C)
        copy = pltpu.make_async_copy(xv, y_hbm, in_sem.at[0])
        copy.start()
        return copy

    if not summed:
        finish(g_copies, gs, gh)
        back(0, R // step)
        y_copy = put()
        a_copy = pltpu.make_async_copy(total, a_hbm, in_sem.at[1])
        a_copy.start()
        a_copy.wait()
        y_copy.wait()
        return

    pairs = D * T // 2
    core = t % 2
    own = d * (T // 2) + t // 2
    half = 8 * F // 2
    piece = half // pairs
    partner = (d, t + 1 - 2 * core)
    theirs = pl.ds(pl.multiple_of((1 - core) * half, half), half)
    mine = pl.ds(pl.multiple_of(core * half, half), half)
    s1[...] = total[theirs, :].astype(bf16)
    first = pltpu.make_async_remote_copy(
        src_ref=s1, dst_ref=r1, send_sem=pair_sem.at[0], recv_sem=pair_sem.at[1],
        device_id=partner, device_id_type=MESH)
    first.start()
    finish(g_copies, gs, gh)
    first.wait()
    s2[...] = (total[mine, :] + r1[...].astype(f32)).astype(bf16)

    def other(s):
        p = lax.rem(own + s, pairs)
        return p, (p // (T // 2), 2 * (p % (T // 2)) + core)

    def rows_of(p):
        return pl.ds(pl.multiple_of(p * piece, piece), piece)

    scatters = []
    for s in range(1, pairs):
        p, device = other(s)
        copy = pltpu.make_async_remote_copy(
            src_ref=s2.at[rows_of(p)], dst_ref=r2.at[own], send_sem=rs_s.at[s], recv_sem=rs_r.at[own],
            device_id=device, device_id_type=MESH)
        copy.start()
        scatters.append(copy)
    r2[own] = s2[rows_of(own), :]
    back(0, R // step)
    y_copy = put()

    for s in range(1, pairs):
        p, device = other(s)
        pltpu.make_async_remote_copy(
            src_ref=s2.at[rows_of(p)], dst_ref=r2.at[p], send_sem=rs_s.at[s], recv_sem=rs_r.at[p],
            device_id=device, device_id_type=MESH).wait_recv()
    ended = r2[0].astype(f32)
    for p in range(1, pairs):
        ended += r2[p].astype(f32)

    def place(p):
        return full.at[pl.ds(pl.multiple_of(core * half + p * piece, piece), piece)]

    full[pl.ds(pl.multiple_of(core * half + own * piece, piece), piece), :] = ended.astype(bf16)
    gathers = []
    for s in range(1, pairs):
        p, device = other(s)
        copy = pltpu.make_async_remote_copy(
            src_ref=place(own), dst_ref=place(own), send_sem=ag_s.at[s], recv_sem=ag_r.at[own],
            device_id=device, device_id_type=MESH)
        copy.start()
        gathers.append(copy)
    for s in range(1, pairs):
        p, device = other(s)
        pltpu.make_async_remote_copy(
            src_ref=place(own), dst_ref=place(p), send_sem=ag_s.at[s], recv_sem=ag_r.at[p],
            device_id=device, device_id_type=MESH).wait_recv()
    last = pltpu.make_async_remote_copy(
        src_ref=full.at[mine], dst_ref=full.at[mine], send_sem=pair_sem.at[2], recv_sem=pair_sem.at[3],
        device_id=partner, device_id_type=MESH)
    last.start()
    for copy in scatters + gathers:
        copy.wait_send()
    last.wait()
    a_copy = pltpu.make_async_copy(full, a_hbm, in_sem.at[1])
    a_copy.start()
    a_copy.wait()
    y_copy.wait()


def on_device(D, T, inputs, cotangent, weight, bias, ocean):
    F, R, C = inputs.shape
    assert C == LANES and F == LANES
    summed = D * T <= SUMMED
    pairs = D * T // 2 if summed else 1
    piece = 4 * F // pairs
    scale = (R * C * D * T) ** -0.5
    mask = jnp.repeat(ocean.astype(f32), BLOCK, 1)
    any_space = pl.BlockSpec(memory_space=pl.ANY)
    vmem = pl.BlockSpec(memory_space=pltpu.VMEM)
    dma = pltpu.SemaphoreType.DMA
    grad_inputs, sums = pl.pallas_call(
        functools.partial(kernel, D, T, R, F, summed),
        out_shape=(
            jax.ShapeDtypeStruct((F, R, C), bf16),
            jax.ShapeDtypeStruct((8 * F, F), bf16 if summed else f32),
        ),
        in_specs=[any_space, any_space, any_space, vmem, vmem],
        out_specs=(any_space, any_space),
        scratch_shapes=[
            pltpu.VMEM((F, R, C), bf16), pltpu.VMEM((F, R, C), bf16), pltpu.VMEM((7, F, F), bf16),
            pltpu.VMEM((F * R, C), f32), pltpu.VMEM((F * R, C), f32),
            pltpu.VMEM((3 * F, (R + 2) * C), bf16), pltpu.VMEM((3 * F, (R + 2) * C), bf16),
            pltpu.VMEM((F, 7 * F), bf16), pltpu.VMEM((F, 7 * F), bf16),
            pltpu.VMEM((F, F), f32), pltpu.VMEM((F, C), f32),
            [pltpu.VMEM((2, F, C), f32), pltpu.VMEM((2, F, C), bf16)],
            [pltpu.VMEM((2, F, C), f32), pltpu.VMEM((2, F, C), bf16)],
            pltpu.VMEM((6, F, C), bf16), pltpu.VMEM((6, F, C), bf16),
            pltpu.VMEM((8 * F, F), f32), pltpu.VMEM((4 * F, F), bf16), pltpu.VMEM((4 * F, F), bf16),
            pltpu.VMEM((4 * F, F), bf16), pltpu.VMEM((pairs, piece, F), bf16), pltpu.VMEM((8 * F, F), bf16),
            dma((3,)), dma((6,)), dma((6,)), dma((6,)), dma((6,)), dma((4,)),
            dma((pairs,)), dma((pairs,)), dma((pairs,)), dma((pairs,)),
        ],
        compiler_params=pltpu.CompilerParams(collective_id=0, has_side_effects=True),
        name="hex_backward",
    )(inputs, cotangent, weight, bias.reshape(1, F), mask)
    if not summed:
        sums = lax.psum(sums, ("diamond", "tile"))
    sums = sums.astype(f32) * scale
    return grad_inputs, sums[:7 * F].reshape(7, F, F), sums[7 * F]


def solution(mesh):
    cells = P(None, "diamond", "tile")
    return jax.shard_map(
        functools.partial(on_device, mesh.shape["diamond"], mesh.shape["tile"]),
        mesh=mesh,
        in_specs=(cells, cells, P(), P(), P("diamond", "tile")),
        out_specs=(cells, P(), P()),
        check_vma=False,
    )
```

time: 197 us -> 46.9 us (0.24)
  blocking collectives: 41.4 us -> 0 us
  Pallas kernels: 0 us -> 41.2 us
  waiting for transfers between devices: 41 us -> 0 us
  local copies, waits for them, and re-layouts: 43.3 us -> 3.68 us
  starting transfers between devices: 23.7 us -> 0 us
  matrix products: 19 us -> 0 us
  between operations: 14.3 us -> 0.66 us
  other arithmetic: 13.6 us -> 1.08 us
    psum x1 -> x0, blocking collectives: 41.4 us -> none  [on_device(): sum_w, sum_b = lax.psum((local_w, local_b), ('diamond', 'tile'))]
    pallas_call x0 -> x1, Pallas kernels: none -> 41.2 us  [on_device(): pl.pallas_call(functools.partial(kernel, D, T, R, F, summed), out_shape=(...]
    psum x1 -> x0, waiting for transfers between devices: 38.9 us -> none  [on_device(): sum_w, sum_b = lax.psum((local_w, local_b), ('diamond', 'tile'))]
    another operation x3 -> x0, local copies, waits for them, and re-layouts: 26 us -> none  [stacked_taps(): return jnp.stack(pieces, 0)]
    ppermute x8 -> x0, starting transfers between devices: 23.7 us -> none  [the longest x4 16.3 us: extended(): before = lax.ppermute(last, axis, up)]
    dot_general x3 -> x0, matrix products: 19 us -> none  [the longest x1 9.47 us: on_device(): total = jnp.dot(back_weight, back_taps, preferred_element_type=jnp.float32)]
    unnamed x29 -> x5, local copies, waits for them, and re-layouts: 13.6 us -> 1.65 us
    unnamed x7 -> x0, other arithmetic: 8.35 us -> none
  transfers between devices with their start and end apart: 9 -> 0, of which waited for: 2 -> 0; matrix products, arithmetic and copies ran while one was open for 21% -> 0% of each run, Pallas kernels for 0% -> 0%
where the time goes in v1:
time: 46.9 us; the launch traced here: 46.7 us
  Pallas kernels  41.2 us (88%)
  local copies, waits for them, and re-layouts  3.68 us (8%)
  other arithmetic  1.08 us (2%)
  between operations  0.66 us (1%)
    pallas_call x1, Pallas kernels, on_device(): pl.pallas_call(functools.partial(kernel, D, T, R, F, summed), out_shape=(...  41.2 us
    unnamed x5, local copies, waits for them, and re-layouts  1.65 us
    mul x1, other arithmetic, on_device(): sums = sums.astype(f32) * scale  1.08 us

profile of v1, /device:TPU:1, one launch (start us, length us, event | category | flops | bytes accessed | tf_op | source)
XLA Modules:
  0.0 46.7 jit_solution(17560779777457244940)
XLA Ops:
  0.6 0.0 copy-start.1
  0.6 0.7 %copy-done.1 = s32[2,8]{1,0:T(2,128)S(1)} copy-done((s32[2,8]{1,0:T(2,128)S(1)}, s32[2,8]{1,0:T(2,128)}, u32[]{:S(2)}) %copy-start.1) | copy-done | bytes 88
  1.3 0.1 broadcast_in_dim.3
  1.4 0.6 %reshape.16.m_ref = f32[2,128]{1,0:T(2,128)} reshape(f32[2,8,16]{2,1,0:T(8,128)S(1)} %broadcast_in_dim.3) | data formatting | bytes 2048 | tf_op jit(solution)/shard_map/reshape | solution.py:295
  2.0 41.2 %hex_backward.1 = (bf16[128,32,128]{2,1,0:T(8,128)(2,1)}, bf16[1024,128]{1,0:T(8,128)(2,1)}) custom-call(bf16[128,32,128]{2,1,0:T(8,128)(2,1)} %x_hbm.1, bf16[128,32,128]{2,1,0:T(8,128)(2,1)} %c_hbm.1, bf16[7,128,128]{2,1,0:T(8,128)(2,1)} %w_hbm.1, f32[1,128]{1,0:T(1,128)} %bitcast.5, f32[2,128]{1,0:T(2,128)} %reshape.16.m_ref), custom_call_target="tpu_custom_call" | custom-call | tf_op jit(solution)/shard_map/hex_backward/pallas_call | solution.py:299
  43.3 0.0 copy-start
  43.3 1.1 %convert_multiply_fusion = f32[1024,128]{1,0:T(8,128)S(1)} fusion(bf16[1024,128]{1,0:T(8,128)(2,1)} %get-tuple-element.6), kind=kLoop, calls=%fused_computation | loop fusion | flops 262144 | bytes 786432 | tf_op jit(solution)/shard_map/mul | solution.py:326
  44.4 0.5 %slice_bitcast_fusion = f32[128]{0:T(128)} fusion(f32[1024,128]{1,0:T(8,128)S(1)} %convert_multiply_fusion), kind=kLoop, calls=%fused_computation.1 | loop fusion | bytes 1024 | tf_op jit(solution)/shard_map/squeeze | solution.py:327
  44.9 0.8 %slice.8 = f32[896,128]{1,0:T(8,128)} slice(f32[1024,128]{1,0:T(8,128)S(1)} %convert_multiply_fusion), slice={[0:896], [0:128]} | slice | bytes 917504 | tf_op jit(solution)/shard_map/slice | solution.py:327
  45.7 0.0 copy-done
  45.7 1.0 %copy.9 = bf16[128,32,128]{2,1,0:T(8,128)(2,1)} copy(bf16[128,32,128]{2,1,0:T(8,128)(2,1)S(1)} %copy-done) | data formatting | bytes 2097152
  (1 shorter events, 0.0 us)
Async XLA Ops:
  0.6 0.7 %copy-start.1 = (s32[2,8]{1,0:T(2,128)S(1)}, s32[2,8]{1,0:T(2,128)}, u32[]{:S(2)}) copy-start(s32[2,8]{1,0:T(2,128)} %param.9) | copy-start | bytes 196
  43.3 2.4 %copy-start = (bf16[128,32,128]{2,1,0:T(8,128)(2,1)S(1)}, bf16[128,32,128]{2,1,0:T(8,128)(2,1)}, u32[]{:S(2)}) copy-start(bf16[128,32,128]{2,1,0:T(8,128)(2,1)} %get-tuple-element.10) | copy-start | bytes 3145732
